TPU v7x, 32 devices: a whole 2x2x4 slice. The times are simulated.
32 devices in a mesh: dom: 8 (over y, x, core), group: 4 (over z).
Axes of the slice: x: 2, y: 2, z: 4, core: 2. Of those that a mesh axis runs over, the one named last changes fastest.
Arguments:
- nodes: bfloat16 [32, 256, 128], P(('dom', 'group')), may hold values from -6 to 6
- edges: bfloat16 [32, 1536, 128], P(('dom', 'group')), may hold values from -6 to 6
- node_cot: bfloat16 [32, 256, 128], P(('dom', 'group')), may hold values from -6 to 6
- send_index: int32 [32, 4, 128], P(('dom', 'group')), may hold values from 0 to 255
- halo_count: int32 [32, 4], P(('dom', 'group')), may hold values from 0 to 128, as said below
- senders: int32 [32, 1536], P(('dom', 'group')), may hold values from 0 to 767, as said below
- receivers: int32 [32, 1536], P(('dom', 'group')), may hold values from 0 to 255, as said below
- edge_in_w: bfloat16 [2, 384, 128], replicated, may hold values from -0.3125 to 0.3125
- edge_out_w: bfloat16 [2, 128, 128], replicated, may hold values from -0.5 to 0.5
- node_in_w: bfloat16 [2, 256, 128], replicated, may hold values from -0.375 to 0.375
- node_out_w: bfloat16 [2, 128, 128], replicated, may hold values from -0.5 to 0.5
- biases: float32 [2, 4, 128], replicated, may hold values from -3 to 3
- gains: float32 [2, 2, 128], replicated, may hold values from 0.1 to 1.9
Outputs:
- nodes_out: bfloat16 [32, 256, 128], P(('dom', 'group'))
- node_grad: bfloat16 [32, 256, 128], P(('dom', 'group'))
- edge_grad: bfloat16 [32, 1536, 128], P(('dom', 'group'))
- edge_in_grad: float32 [2, 384, 128], replicated
- edge_out_grad: float32 [2, 128, 128], replicated
- node_in_grad: float32 [2, 256, 128], replicated
- node_out_grad: float32 [2, 128, 128], replicated
- bias_grad: float32 [2, 4, 128], replicated
- gain_grad: float32 [2, 2, 128], replicated
Inputs may be any that keep to these rules, and one draw needn't show every extreme that they name: `halo_count`: slot order: from the lower then the upper partition along dom, then along group; 0 exactly where that neighbour does not exist; every slot reaches 128 on some partition. `senders`: below 256: a node of the partition; 256 + s: the s-th live halo row of the table, s below the partition's total halo_count. `receivers`: never fall along a partition's edges; within each aligned block of 512 edges they span fewer than 128 nodes.
All inputs are finite; a program needn't handle non-finite values.
Results may differ from a plain program's by a relative error of at most 0.02.
Values may be sent and summed in bfloat16 or wider, within the bound.
A program may use at most 64 MiB of HBM per device.

v0:
```python
import jax
import jax.numpy as jnp
from jax import lax
from jax.sharding import PartitionSpec as P


def padded(x, sides, width):
    for axis, dim in sides:
        size, length = (lax.axis_size(axis), x.shape[dim])
        up = [(i, (i + 1) % size) for i in range(size - 1)]
        down = [(j, i) for i, j in up]
        last = lax.slice_in_dim(x, length - width, length, axis=dim)
        first = lax.slice_in_dim(x, 0, width, axis=dim)
        before = lax.ppermute(last, axis, up)
        after = lax.ppermute(first, axis, down)
        x = jnp.concatenate([before, x, after], axis=dim)
    return x


def norm_rows(values, gain_row):
    centre = values - jnp.mean(values, axis=-1, keepdims=True)
    spread = jnp.mean(centre * centre, axis=-1, keepdims=True)
    return centre * lax.rsqrt(spread + 1e-05) * gain_row


def pack_halo(received, counts):
    halo_depth = received.shape[1]
    feat_width = received.shape[2]
    block_ends = jnp.cumsum(counts)
    block_starts = block_ends - counts
    positions = jnp.arange(4 * halo_depth, dtype=jnp.int32)
    block_of = jnp.sum((positions[:, None] >= block_ends[None, :]).astype(jnp.int32), axis=1)
    clamped = jnp.minimum(block_of, 3)
    selector = jnp.arange(4, dtype=jnp.int32)
    offsets = jnp.sum(
        jnp.where(clamped[:, None] == selector[None, :], block_starts[None, :], 0), axis=1
    )
    within_block = positions - offsets
    sources = clamped * halo_depth + jnp.clip(within_block, 0, halo_depth - 1)
    picked = received.reshape(4 * halo_depth, feat_width)[sources]
    return jnp.where((block_of < 4)[:, None], picked, jnp.zeros_like(picked))


def edge_update(weights, edge_rows, sent_feat, recv_feat):
    edge_in, edge_out, node_in, node_out, bias_rows, gain_rows = weights
    joined = jnp.concatenate([edge_rows, sent_feat, recv_feat], axis=1)
    hidden = jax.nn.silu(
        jnp.dot(joined, edge_in, preferred_element_type=jnp.float32) + bias_rows[0]
    ).astype(jnp.bfloat16)
    mapped = jnp.dot(hidden, edge_out, preferred_element_type=jnp.float32) + bias_rows[1]
    return (edge_rows.astype(jnp.float32) + norm_rows(mapped, gain_rows[0])).astype(jnp.bfloat16)


def node_update(weights, node_vals, summed):
    edge_in, edge_out, node_in, node_out, bias_rows, gain_rows = weights
    joined = jnp.concatenate([node_vals.astype(jnp.bfloat16), summed.astype(jnp.bfloat16)], axis=1)
    hidden = jax.nn.silu(
        jnp.dot(joined, node_in, preferred_element_type=jnp.float32) + bias_rows[2]
    ).astype(jnp.bfloat16)
    mapped = jnp.dot(hidden, node_out, preferred_element_type=jnp.float32) + bias_rows[3]
    return (node_vals + norm_rows(mapped, gain_rows[1])).astype(jnp.bfloat16)


def aggregate(edge_new, receiver_ids, node_count):
    block_count = edge_new.shape[0] // 512
    window = jnp.arange(256, dtype=jnp.int32)
    totals = jnp.zeros((node_count, edge_new.shape[1]), jnp.float32)

    def add_block(block_index, running):
        first_edge = block_index * 512
        block_rows = lax.dynamic_slice_in_dim(edge_new, first_edge, 512, 0)
        targets = lax.dynamic_slice_in_dim(receiver_ids, first_edge, 512, 0)
        window_start = jnp.minimum(targets[0] // 128 * 128, node_count - 256)
        onehot = ((targets - window_start)[:, None] == window[None, :]).astype(jnp.bfloat16)
        partial_sum = lax.dot_general(
            onehot, block_rows, (((0,), (0,)), ((), ())), preferred_element_type=jnp.float32
        )
        return running + partial_sum

    return lax.fori_loop(0, block_count, add_block, totals)


def local_layer(weights, edge_rows, node_vals, received, counts, sender_ids, receiver_ids):
    table = jnp.concatenate([node_vals, pack_halo(received, counts)], axis=0)
    sent_feat = table[sender_ids].astype(jnp.bfloat16)
    recv_feat = table[receiver_ids].astype(jnp.bfloat16)
    edge_new = edge_update(weights, edge_rows, sent_feat, recv_feat)
    summed = aggregate(edge_new, receiver_ids, node_vals.shape[0])
    return (edge_new, node_update(weights, node_vals, summed))


def fetch_rows(node_rows, send_rows):
    blocks = node_rows[send_rows]
    extended = padded(jnp.stack([blocks[1], blocks[0]]), (("dom", 0),), 1)
    across = padded(jnp.stack([blocks[3], blocks[2]]), (("group", 0),), 1)
    return jnp.stack([extended[0], extended[3], across[0], across[3]]).astype(jnp.float32)


def return_rows(halo_cot, send_rows, node_count):
    extended = padded(
        jnp.stack([halo_cot[0], halo_cot[1]]).astype(jnp.bfloat16), (("dom", 0),), 1
    ).astype(jnp.float32)
    across = padded(
        jnp.stack([halo_cot[2], halo_cot[3]]).astype(jnp.bfloat16), (("group", 0),), 1
    ).astype(jnp.float32)
    returned = jnp.stack([extended[3], extended[0], across[3], across[0]])
    return jax.ops.segment_sum(
        returned.reshape(-1, returned.shape[-1]), send_rows.reshape(-1), num_segments=node_count
    )


def reduce_grads(stacked):
    flattened = jnp.concatenate([member.reshape(-1) for member in stacked])
    shares = lax.psum_scatter(
        flattened.astype(jnp.bfloat16), "dom", scatter_dimension=0, tiled=True
    ).astype(jnp.float32)
    shares = lax.psum(shares, "group")
    whole_vector = lax.all_gather(shares, "dom", axis=0, tiled=True)
    pieces = []
    cursor = 0
    for member in stacked:
        pieces.append(whole_vector[cursor : cursor + member.size].reshape(member.shape))
        cursor = cursor + member.size
    return tuple(pieces)


def shards(
    nodes,
    edges,
    node_cot,
    send_index,
    halo_count,
    senders,
    receivers,
    edge_in_w,
    edge_out_w,
    node_in_w,
    node_out_w,
    biases,
    gains,
):
    node_rows = nodes[0]
    edge_rows = edges[0]
    send_rows = send_index[0]
    counts = halo_count[0]
    sender_ids = senders[0]
    receiver_ids = receivers[0]
    layer_count = edge_in_w.shape[0]
    node_count = node_rows.shape[0]

    def layer_call(params, edge_arg, node_arg, halo_arg):
        return local_layer(params, edge_arg, node_arg, halo_arg, counts, sender_ids, receiver_ids)

    pullbacks = []
    for layer_index in range(layer_count):
        weights = (
            edge_in_w[layer_index],
            edge_out_w[layer_index],
            node_in_w[layer_index],
            node_out_w[layer_index],
            biases[layer_index],
            gains[layer_index],
        )
        received = fetch_rows(node_rows, send_rows)
        (edge_rows, node_rows), pullback = jax.vjp(
            layer_call, weights, edge_rows, node_rows.astype(jnp.float32), received
        )
        pullbacks.append(pullback)
    node_grad_rows = node_cot[0]
    edge_grad_rows = jnp.zeros_like(edges[0])
    layer_grads = [None] * layer_count
    for layer_index in reversed(range(layer_count)):
        weight_cot, edge_grad_rows, node_vals_cot, halo_cot = pullbacks[layer_index](
            (edge_grad_rows, node_grad_rows)
        )
        node_vals_cot = node_vals_cot + return_rows(halo_cot, send_rows, node_count)
        node_grad_rows = node_vals_cot.astype(jnp.bfloat16)
        layer_grads[layer_index] = [leaf_val.astype(jnp.float32) for leaf_val in weight_cot]
    stacked = tuple(
        (
            jnp.stack([layer_grads[layer_index][member] for layer_index in range(layer_count)])
            for member in range(6)
        )
    )
    summed = reduce_grads(stacked)
    grad_scale = (lax.axis_size("dom") * lax.axis_size("group") * node_count) ** (-0.5)
    scaled = [member * grad_scale for member in summed]
    return (
        node_rows[None],
        node_grad_rows[None],
        edge_grad_rows[None],
        scaled[0],
        scaled[1],
        scaled[2],
        scaled[3],
        scaled[4],
        scaled[5],
    )


def solution(mesh):
    in_specs = (
        P(("dom", "group"), None, None),
        P(("dom", "group"), None, None),
        P(("dom", "group"), None, None),
        P(("dom", "group"), None, None),
        P(("dom", "group"), None),
        P(("dom", "group"), None),
        P(("dom", "group"), None),
        P(),
        P(),
        P(),
        P(),
        P(),
        P(),
    )
    out_specs = (
        P(("dom", "group"), None, None),
        P(("dom", "group"), None, None),
        P(("dom", "group"), None, None),
        P(),
        P(),
        P(),
        P(),
        P(),
        P(),
    )
    return jax.shard_map(shards, mesh=mesh, in_specs=in_specs, out_specs=out_specs, check_vma=False)
```

profile of v0, /device:TPU:0, one launch (start us, length us, event | category | flops | bytes accessed | tf_op | source)
XLA Modules:
  0.0 406.8 jit_solution(6415277508827828346)
XLA Ops:
  12.4 4.3 %collective-permute-start.2 = (bf16[1,128,128]{2,1,0:T(8,128)(2,1)S(1)}, bf16[1,128,128]{2,1,0:T(8,128)(2,1)S(1)}, u32[]{:S(2)}, u32[]{:S(2)}) collective-permute-start(bf16[1,128,128]{2,1,0:T(8,128)(2,1)S(1)} %get-tuple-element.934), channel_id=1, source_target_pairs={{0,1},{1,2},{2,3},{4,5},{5,6},{6,7},{8,9},{9,10},{10,11},{12,13},{... | collective-permute-start | bytes 98312 | tf_op jit(solution)/shard_map/ppermute | solution.py:14
  28.9 3.2 gather_fusion.2
  34.9 15.4 %while.72 = (s32[]{:T(128)}, f32[256,128]{1,0:T(8,128)S(1)}, s32[3]{0:T(128)}, bf16[3,512,256]{2,1,0:T(8,128)(2,1)S(1)}, s32[1536]{0:T(1024)S(1)}, /*index=5*/bf...) while((s32[]{:T(128)}, f32[256,128]{1,0:T(8,128)S(1)}, ...), condition=%wide.region_6.7_spmd.clone.clone, body=%wide.region_5.6_spmd.clone.clone.sunk | while | flops 34013720 | bytes 668059 | solution.py:80
  57.3 3.5 collective-permute-start.6
  72.8 3.2 gather_fusion.6
  79.7 23.8 %while.73 = (s32[]{:T(128)}, f32[256,128]{1,0:T(8,128)}, s32[3]{0:T(128)}, bf16[3,512,256]{2,1,0:T(8,128)(2,1)S(1)}, s32[1536]{0:T(1024)}, /*index=5*/bf16[1536,...) while((s32[]{:T(128)}, f32[256,128]{1,0:T(8,128)}, ...), condition=%wide.region_12.13_spmd.clone.clone, body=%wide.region_11.12_spmd.clone.clone.sunk | while | flops 34013720 | bytes 668567 | solution.py:80
  112.6 14.7 %while.70 = (s32[]{:T(128)}, bf16[1536,128]{0,1:T(8,128)(2,1)S(1)}, s32[3]{0:T(128)}, bf16[3,512,256]{2,1,0:T(8,128)(2,1)}, bf16[256,128]{1,0:T(8,128)(2,1)}, /*index=5*/s32[]{:T(128)}, s32[]{:T(128)}, s32[]{:T(128)}) while((s32[]{:T(128)}, bf16[1536,128]{0,1:T(8,128)(2,1)S(1)}, s32[3]{0:T(128)}, bf16[3,512,256]{2,1,0:T(8,128)(2,1)}, ...), condition=%wide.region_18.19_spmd, body=%wide.region_17.18_spmd.sunk | while | flops 33619968 | bytes 1638521 | solution.py:80
  136.4 9.7 %scatter_custom_fusion.1 = f32[768,128]{1,0:T(8,128)S(1)} fusion(s32[1536]{0:T(1024)} %copy-done.61, f32[1536,128]{1,0:T(8,128)} %copy.168, f32[]{:T(128)} %constant.293.clone.1), kind=kCustom, calls=%fused_computation.153 | custom fusion | flops 196608 | bytes 393728 | tf_op jit(solution)/shard_map/transpose(jvp())/scatter-add | solution.py:85
  148.6 10.5 %scatter_custom_fusion = f32[768,128]{1,0:T(8,128)S(1)} fusion(s32[1536]{0:T(1024)} %copy-done.60, f32[1536,128]{1,0:T(8,128)} %copy.167, f32[]{:T(128)} %constant.293.clone.1), kind=kCustom, calls=%fused_computation.155 | custom fusion | flops 196608 | bytes 393728 | tf_op jit(solution)/shard_map/transpose(jvp())/scatter-add | solution.py:86
  162.3 3.5 scatter_custom_fusion.2
  167.1 4.5 %collective-permute-start.10 = (bf16[1,128,128]{2,1,0:T(8,128)(2,1)S(1)}, bf16[1,128,128]{2,1,0:T(8,128)(2,1)S(1)}, u32[]{:S(2)}, u32[]{:S(2)}) collective-permute-start(bf16[1,128,128]{2,1,0:T(8,128)(2,1)S(1)} %get-tuple-element.925), channel_id=1, source_target_pairs={{0,1},{1,2},{2,3},{4,5},{5,6},{6,7},{8,9},{9,10},{10,11},{12,13},{... | collective-permute-start | bytes 98312 | tf_op jit(solution)/shard_map/ppermute | solution.py:14
  173.3 3.4 collective-permute-start.8
  178.9 3.6 collective-permute-done.9
  182.6 3.5 scatter_fusion
  191.6 14.8 %while.71 = (s32[]{:T(128)}, bf16[1536,128]{0,1:T(8,128)(2,1)S(1)}, s32[3]{0:T(128)}, bf16[3,512,256]{2,1,0:T(8,128)(2,1)S(1)}, bf16[256,128]{1,0:T(8,128)(2,1)}, /*index=5*/s32[]{:T(128)}, s32[]{:T(128)}, s32[]{:T(128)}) while((s32[]{:T(128)}, bf16[1536,128]{0,1:T(8,128)(2,1)S(1)}, s32[3]{0:T(128)}, bf16[3,512,256]{2,1,0:T(8,128)(2,1)S(1)}, ...), condition=%wide.region_28.29_spmd, body=%wide.region_27.28_spmd.sunk | while | flops 33619968 | bytes 1638521 | solution.py:80
  214.8 9.2 %scatter_custom_fusion.5 = f32[768,128]{1,0:T(8,128)S(1)} fusion(s32[1536]{0:T(1024)} %copy-done.61, f32[1536,128]{1,0:T(8,128)} %copy.181, f32[]{:T(128)} %constant.293.clone.1), kind=kCustom, calls=%fused_computation.149 | custom fusion | flops 196608 | bytes 393728 | tf_op jit(solution)/shard_map/transpose(jvp())/scatter-add | solution.py:85
  225.4 10.6 %scatter_custom_fusion.4 = f32[768,128]{1,0:T(8,128)S(1)} fusion(s32[1536]{0:T(1024)} %copy-done.60, f32[1536,128]{1,0:T(8,128)} %copy.180, f32[]{:T(128)} %constant.293.clone.1), kind=kCustom, calls=%fused_computation.151 | custom fusion | flops 196608 | bytes 393728 | tf_op jit(solution)/shard_map/transpose(jvp())/scatter-add | solution.py:86
  239.1 3.5 scatter_custom_fusion.6
  242.7 4.7 %collective-permute-start.12 = (bf16[1,128,128]{2,1,0:T(8,128)(2,1)S(1)}, bf16[1,128,128]{2,1,0:T(8,128)(2,1)S(1)}, u32[]{:S(2)}, u32[]{:S(2)}) collective-permute-start(bf16[1,128,128]{2,1,0:T(8,128)(2,1)S(1)} %get-tuple-element.915), channel_id=1, source_target_pairs={{0,4},{4,8},{8,12},{12,16},{16,20},{20,24},{24,28},{1,5},{5,9},{9,... | collective-permute-start | bytes 98312 | tf_op jit(solution)/shard_map/ppermute | solution.py:14
  248.7 4.5 %collective-permute-start.14 = (bf16[1,128,128]{2,1,0:T(8,128)(2,1)S(1)}, bf16[1,128,128]{2,1,0:T(8,128)(2,1)S(1)}, u32[]{:S(2)}, u32[]{:S(2)}) collective-permute-start(bf16[1,128,128]{2,1,0:T(8,128)(2,1)S(1)} %get-tuple-element.917), channel_id=1, source_target_pairs={{0,1},{1,2},{2,3},{4,5},{5,6},{6,7},{8,9},{9,10},{10,11},{12,13},{... | collective-permute-start | bytes 98312 | tf_op jit(solution)/shard_map/ppermute | solution.py:14
  254.6 40.7 %all-reduce.22.cloned.1.call-done = bf16[230912]{0:T(1024)(128)(2,1)} async-done(((bf16[230912]{0:T(1024)(128)(2,1)}), bf16[230912]{0:T(1024)(128)(2,1)}) %all-reduce.22.cloned.1.call-update) | async-done | bytes 461840
  297.0 35.8 %all-reduce.18.cloned.1.call-done = f32[28864]{0:T(1024)} async-done(((f32[28864]{0:T(1024)}), f32[28864]{0:T(1024)}) %all-reduce.18.cloned.1.call-update) | async-done | bytes 115472 | tf_op jit(solution)/shard_map/psum | solution.py:117
  335.3 3.4 scatter_fusion.1
  339.3 53.0 %all-reduce.20.cloned.1.call-done = f32[230912]{0:T(1024)} async-done(((f32[230912]{0:T(1024)}), f32[230912]{0:T(1024)}) %all-reduce.20.cloned.1.call-update) | async-done | bytes 923664
  (513 shorter events, 155.1 us)
Async XLA Ops:
  7.2 288.1 %all-reduce.22.cloned.1.call-start = ((), (), s32[]{:S(2)}) async-start(), calls=%async_computation.2 | async-start | bytes 925696
  10.0 11.7 %collective-permute-start = (bf16[1,128,128]{2,1,0:T(8,128)(2,1)S(1)}, bf16[1,128,128]{2,1,0:T(8,128)(2,1)S(1)}, u32[]{:S(2)}, u32[]{:S(2)}) collective-permute-start(bf16[1,128,128]{2,1,0:T(8,128)(2,1)S(1)} %get-tuple-element.933), channel_id=1, source_target_pairs={{0,4},{4,8},{8,12},{12,16},{16,20},{20,24},{24,28},{1,5},{5,9},{9,... | collective-permute-start | bytes 98312 | tf_op jit(solution)/shard_map/ppermute | solution.py:14
  12.4 9.3 %collective-permute-start.2 = (bf16[1,128,128]{2,1,0:T(8,128)(2,1)S(1)}, bf16[1,128,128]{2,1,0:T(8,128)(2,1)S(1)}, u32[]{:S(2)}, u32[]{:S(2)}) collective-permute-start(bf16[1,128,128]{2,1,0:T(8,128)(2,1)S(1)} %get-tuple-element.934), channel_id=1, source_target_pairs={{0,1},{1,2},{2,3},{4,5},{5,6},{6,7},{8,9},{9,10},{10,11},{12,13},{... | collective-permute-start | bytes 98312 | tf_op jit(solution)/shard_map/ppermute | solution.py:14
  16.7 5.0 %collective-permute-start.1 = (bf16[1,128,128]{2,1,0:T(8,128)(2,1)S(1)}, bf16[1,128,128]{2,1,0:T(8,128)(2,1)S(1)}, u32[]{:S(2)}, u32[]{:S(2)}) collective-permute-start(bf16[1,128,128]{2,1,0:T(8,128)(2,1)S(1)} %get-tuple-element.935), channel_id=1, source_target_pairs={{4,0},{8,4},{12,8},{16,12},{20,16},{24,20},{28,24},{5,1},{9,5},{13... | collective-permute-start | bytes 98312 | tf_op jit(solution)/shard_map/ppermute | solution.py:15
  18.0 5.8 %collective-permute-start.3 = (bf16[1,128,128]{2,1,0:T(8,128)(2,1)S(1)}, bf16[1,128,128]{2,1,0:T(8,128)(2,1)S(1)}, u32[]{:S(2)}, u32[]{:S(2)}) collective-permute-start(bf16[1,128,128]{2,1,0:T(8,128)(2,1)S(1)} %get-tuple-element.936), channel_id=1, source_target_pairs={{1,0},{2,1},{3,2},{5,4},{6,5},{7,6},{9,8},{10,9},{11,10},{13,12},{... | collective-permute-start | bytes 98312 | tf_op jit(solution)/shard_map/ppermute | solution.py:15
  19.6 49.8 %copy-start.73 = (pred[512]{0:T(512)(128)(4,1)}, pred[512]{0:T(512)(128)(4,1)S(1)}, u32[]{:S(2)}) copy-start(pred[512]{0:T(512)(128)(4,1)S(1)} %broadcast_compare_fusion) | copy-start | bytes 1540
  20.1 32.1 %copy-start.76 = (f32[128]{0:T(128)}, f32[128]{0:T(128)S(1)}, u32[]{:S(2)}) copy-start(f32[128]{0:T(128)S(1)} %get-tuple-element.948) | copy-start | bytes 1540
  21.5 30.8 %copy-start.18 = (bf16[1,256,128]{1,2,0:T(8,128)(2,1)}, bf16[1,256,128]{1,2,0:T(8,128)(2,1)S(1)}, u32[]{:S(2)}) copy-start(bf16[1,256,128]{1,2,0:T(8,128)(2,1)S(1)} %copy.144) | copy-start | bytes 196612
  34.9 16.4 %copy-start.107 = (bf16[2,128,128]{2,1,0:T(8,128)(2,1)S(1)}, bf16[2,128,128]{2,1,0:T(8,128)(2,1)}, u32[]{:S(2)}) copy-start(bf16[2,128,128]{2,1,0:T(8,128)(2,1)} %param.31) | copy-start | bytes 196612
  52.9 16.5 %copy-start.15 = (bf16[256,128]{0,1:T(8,128)(2,1)}, bf16[256,128]{0,1:T(8,128)(2,1)S(1)}, u32[]{:S(2)}) copy-start(bf16[256,128]{0,1:T(8,128)(2,1)S(1)} %add_convert_fusion.3) | copy-start | bytes 196612
  54.4 11.9 %collective-permute-start.4 = (bf16[1,128,128]{2,1,0:T(8,128)(2,1)S(1)}, bf16[1,128,128]{2,1,0:T(8,128)(2,1)S(1)}, u32[]{:S(2)}, u32[]{:S(2)}) collective-permute-start(bf16[1,128,128]{2,1,0:T(8,128)(2,1)S(1)} %get-tuple-element.929), channel_id=1, source_target_pairs={{0,4},{4,8},{8,12},{12,16},{16,20},{20,24},{24,28},{1,5},{5,9},{9,... | collective-permute-start | bytes 98312 | tf_op jit(solution)/shard_map/ppermute | solution.py:14
  57.3 9.1 %collective-permute-start.6 = (bf16[1,128,128]{2,1,0:T(8,128)(2,1)S(1)}, bf16[1,128,128]{2,1,0:T(8,128)(2,1)S(1)}, u32[]{:S(2)}, u32[]{:S(2)}) collective-permute-start(bf16[1,128,128]{2,1,0:T(8,128)(2,1)S(1)} %get-tuple-element.930), channel_id=1, source_target_pairs={{0,1},{1,2},{2,3},{4,5},{5,6},{6,7},{8,9},{9,10},{10,11},{12,13},{... | collective-permute-start | bytes 98312 | tf_op jit(solution)/shard_map/ppermute | solution.py:14
  60.8 5.6 %collective-permute-start.5 = (bf16[1,128,128]{2,1,0:T(8,128)(2,1)S(1)}, bf16[1,128,128]{2,1,0:T(8,128)(2,1)S(1)}, u32[]{:S(2)}, u32[]{:S(2)}) collective-permute-start(bf16[1,128,128]{2,1,0:T(8,128)(2,1)S(1)} %get-tuple-element.931), channel_id=1, source_target_pairs={{4,0},{8,4},{12,8},{16,12},{20,16},{24,20},{28,24},{5,1},{9,5},{13... | collective-permute-start | bytes 98312 | tf_op jit(solution)/shard_map/ppermute | solution.py:15
  62.1 5.8 %collective-permute-start.7 = (bf16[1,128,128]{2,1,0:T(8,128)(2,1)S(1)}, bf16[1,128,128]{2,1,0:T(8,128)(2,1)S(1)}, u32[]{:S(2)}, u32[]{:S(2)}) collective-permute-start(bf16[1,128,128]{2,1,0:T(8,128)(2,1)S(1)} %get-tuple-element.932), channel_id=1, source_target_pairs={{1,0},{2,1},{3,2},{5,4},{6,5},{7,6},{9,8},{10,9},{11,10},{13,12},{... | collective-permute-start | bytes 98312 | tf_op jit(solution)/shard_map/ppermute | solution.py:15
  165.8 13.0 %collective-permute-start.11 = (bf16[1,128,128]{2,1,0:T(8,128)(2,1)S(1)}, bf16[1,128,128]{2,1,0:T(8,128)(2,1)S(1)}, u32[]{:S(2)}, u32[]{:S(2)}) collective-permute-start(bf16[1,128,128]{2,1,0:T(8,128)(2,1)S(1)} %get-tuple-element.924), channel_id=1, source_target_pairs={{1,0},{2,1},{3,2},{5,4},{6,5},{7,6},{9,8},{10,9},{11,10},{13,12},{... | collective-permute-start | bytes 98312 | tf_op jit(solution)/shard_map/ppermute | solution.py:15
  167.1 11.8 %collective-permute-start.10 = (bf16[1,128,128]{2,1,0:T(8,128)(2,1)S(1)}, bf16[1,128,128]{2,1,0:T(8,128)(2,1)S(1)}, u32[]{:S(2)}, u32[]{:S(2)}) collective-permute-start(bf16[1,128,128]{2,1,0:T(8,128)(2,1)S(1)} %get-tuple-element.925), channel_id=1, source_target_pairs={{0,1},{1,2},{2,3},{4,5},{5,6},{6,7},{8,9},{9,10},{10,11},{12,13},{... | collective-permute-start | bytes 98312 | tf_op jit(solution)/shard_map/ppermute | solution.py:14
  173.3 5.6 %collective-permute-start.8 = (bf16[1,128,128]{2,1,0:T(8,128)(2,1)S(1)}, bf16[1,128,128]{2,1,0:T(8,128)(2,1)S(1)}, u32[]{:S(2)}, u32[]{:S(2)}) collective-permute-start(bf16[1,128,128]{2,1,0:T(8,128)(2,1)S(1)} %get-tuple-element.923), channel_id=1, source_target_pairs={{0,4},{4,8},{8,12},{12,16},{16,20},{20,24},{24,28},{1,5},{5,9},{9,... | collective-permute-start | bytes 98312 | tf_op jit(solution)/shard_map/ppermute | solution.py:14
  176.7 5.8 %collective-permute-start.9 = (bf16[1,128,128]{2,1,0:T(8,128)(2,1)S(1)}, bf16[1,128,128]{2,1,0:T(8,128)(2,1)S(1)}, u32[]{:S(2)}, u32[]{:S(2)}) collective-permute-start(bf16[1,128,128]{2,1,0:T(8,128)(2,1)S(1)} %get-tuple-element.926), channel_id=1, source_target_pairs={{4,0},{8,4},{12,8},{16,12},{20,16},{24,20},{28,24},{5,1},{9,5},{13... | collective-permute-start | bytes 98312 | tf_op jit(solution)/shard_map/ppermute | solution.py:15
  238.0 94.8 %all-reduce.18.cloned.1.call-start = ((), (), s32[]{:S(2)}) async-start(), calls=%async_computation | async-start | bytes 237568 | tf_op jit(solution)/shard_map/psum | solution.py:117
  242.7 92.6 %collective-permute-start.12 = (bf16[1,128,128]{2,1,0:T(8,128)(2,1)S(1)}, bf16[1,128,128]{2,1,0:T(8,128)(2,1)S(1)}, u32[]{:S(2)}, u32[]{:S(2)}) collective-permute-start(bf16[1,128,128]{2,1,0:T(8,128)(2,1)S(1)} %get-tuple-element.915), channel_id=1, source_target_pairs={{0,4},{4,8},{8,12},{12,16},{16,20},{20,24},{24,28},{1,5},{5,9},{9,... | collective-permute-start | bytes 98312 | tf_op jit(solution)/shard_map/ppermute | solution.py:14
  247.4 49.6 %collective-permute-start.15 = (bf16[1,128,128]{2,1,0:T(8,128)(2,1)S(1)}, bf16[1,128,128]{2,1,0:T(8,128)(2,1)S(1)}, u32[]{:S(2)}, u32[]{:S(2)}) collective-permute-start(bf16[1,128,128]{2,1,0:T(8,128)(2,1)S(1)} %get-tuple-element.916), channel_id=1, source_target_pairs={{1,0},{2,1},{3,2},{5,4},{6,5},{7,6},{9,8},{10,9},{11,10},{13,12},{... | collective-permute-start | bytes 98312 | tf_op jit(solution)/shard_map/ppermute | solution.py:15
  248.7 48.3 %collective-permute-start.14 = (bf16[1,128,128]{2,1,0:T(8,128)(2,1)S(1)}, bf16[1,128,128]{2,1,0:T(8,128)(2,1)S(1)}, u32[]{:S(2)}, u32[]{:S(2)}) collective-permute-start(bf16[1,128,128]{2,1,0:T(8,128)(2,1)S(1)} %get-tuple-element.917), channel_id=1, source_target_pairs={{0,1},{1,2},{2,3},{4,5},{5,6},{6,7},{8,9},{9,10},{10,11},{12,13},{... | collective-permute-start | bytes 98312 | tf_op jit(solution)/shard_map/ppermute | solution.py:14
  253.2 82.0 %collective-permute-start.13 = (bf16[1,128,128]{2,1,0:T(8,128)(2,1)S(1)}, bf16[1,128,128]{2,1,0:T(8,128)(2,1)S(1)}, u32[]{:S(2)}, u32[]{:S(2)}) collective-permute-start(bf16[1,128,128]{2,1,0:T(8,128)(2,1)S(1)} %get-tuple-element.918), channel_id=1, source_target_pairs={{4,0},{8,4},{12,8},{16,12},{20,16},{24,20},{28,24},{5,1},{9,5},{13... | collective-permute-start | bytes 98312 | tf_op jit(solution)/shard_map/ppermute | solution.py:15
  296.9 95.5 %all-reduce.20.cloned.1.call-start = ((), (), s32[]{:S(2)}) async-start(), calls=%async_computation.1 | async-start | bytes 1851392
  (116 other events, 416.4 us)
Sparse Core Ops, SparseCore 0:
  238.1 57.1 all-reduce.21
  298.2 34.5 all-reduce.17
  336.1 56.2 all-reduce.19
where the time goes:
time: 414 us; the launch traced here: 407 us
  waiting for transfers between devices  137 us (33%)
  local copies, waits for them, and re-layouts  84.7 us (20%)
  other arithmetic  79.1 us (19%)
  starting transfers between devices  41 us (10%)
  matrix products  32 us (8%)
  between operations  17.6 us (4%)
  loops' own time  15.7 us (4%)
    unnamed x5, waiting for transfers between devices  93.8 us
    psum x1, waiting for transfers between devices, reduce_grads(): shares = lax.psum(shares, 'group')  35.8 us
    ppermute x8, starting transfers between devices, padded(): before = lax.ppermute(last, axis, up)  30.2 us
    scatter-add x2, other arithmetic, local_layer(): recv_feat = table[receiver_ids].astype(jnp.bfloat16)  21.1 us
    scatter-add x2, other arithmetic, local_layer(): sent_feat = table[sender_ids].astype(jnp.bfloat16)  19 us
    another operation x4, loops' own time, aggregate(): return lax.fori_loop(0, block_count, add_block, totals)  15.7 us
    unnamed x255, local copies, waits for them, and re-layouts  14.5 us
    dot_general x12, matrix products, add_block(): lax.dot_general(onehot, block_rows, (((0,), (0,)), ((), ())), preferred_e...  14.2 us
  transfers between devices with their start and end apart: 19, of which 6 were waited for; matrix products, arithmetic and copies ran while one was open for 4% of the time, Pallas kernels for 0%

commit v1 on v0

v1 whole, which is shorter than its diff:
```python
import functools

import jax
import jax.numpy as jnp
from jax import lax
from jax.experimental import pallas as pl
from jax.experimental.pallas import tpu as pltpu
from jax.sharding import PartitionSpec as P

F32 = jnp.float32
BF16 = jnp.bfloat16
MESH = pl.DeviceIdType.MESH


def mm(a, b):
    return lax.dot_general(a, b, (((1,), (0,)), ((), ())), preferred_element_type=F32)


def mm_nt(a, b):
    return lax.dot_general(a, b, (((1,), (1,)), ((), ())), preferred_element_type=F32)


def fold(x):
    return jnp.sum(x.reshape(x.shape[0] // 8, 8, x.shape[1]), axis=0)


def row_sum(x):
    return jnp.sum(x, axis=0, keepdims=True)


def norm_parts(values):
    centre = values - jnp.mean(values, axis=-1, keepdims=True)
    spread = jnp.mean(centre * centre, axis=-1, keepdims=True)
    inv = lax.rsqrt(spread + 1e-05)
    return centre * inv, inv


def norm_back(cot, gain_row, hat, inv):
    u = cot * gain_row
    return inv * (
        u
        - jnp.mean(u, axis=-1, keepdims=True)
        - hat * jnp.mean(u * hat, axis=-1, keepdims=True)
    )


def silu_parts(pre):
    sig = 1.0 / (1.0 + jnp.exp(-pre))
    return (pre * sig).astype(BF16), sig * (1.0 + pre * (1.0 - sig))


def kernel(
    dims,
    cnt,
    nodes,
    edges,
    ncot,
    sidx,
    snd,
    rcv,
    w1,
    w2,
    n1,
    n2,
    bias,
    gain,
    x_out,
    x_grad,
    e_grad,
    g_w1,
    g_w2,
    g_n1,
    g_n2,
    g_b,
    g_g,
    o_s,
    ot_s,
    o_r,
    ot_r,
    o_x,
    ot_x,
    tab,
    e_in,
    e_last,
    sq,
    hid,
    slope,
    hat,
    inv,
    jn,
    nhid,
    nslope,
    nhat,
    ninv,
    dm,
    dp,
    de,
    dsq,
    dx,
    dab,
    fsrc,
    bsrc,
    ret,
    grads,
    buf_a,
    buf_b,
    gat,
    fs,
    fr,
    bs,
    br,
    a_s,
    a_r,
    b_s,
    b_r,
    c_s,
    c_r,
):
    D, G, L, N, E, H, HALO, C, share = dims
    d = lax.axis_index("dom")
    g = lax.axis_index("group")
    rows_w = 7 * H

    has_up = d + 1 < D
    has_down = d > 0
    has_right = g + 1 < G
    has_left = g > 0
    out_ok = (has_up, has_down, has_right, has_left)
    in_ok = (has_down, has_up, has_left, has_right)
    out_dev = ({"dom": d + 1}, {"dom": d - 1}, {"group": g + 1}, {"group": g - 1})
    in_dev = ({"dom": d - 1}, {"dom": d + 1}, {"group": g - 1}, {"group": g + 1})

    def fcopy(l, k):
        return pltpu.make_async_remote_copy(
            src_ref=fsrc.at[l, pl.ds(k * HALO, HALO)],
            dst_ref=tab.at[l, pl.ds(N + k * HALO, HALO)],
            send_sem=fs.at[l, k],
            recv_sem=fr.at[l, k],
            device_id=out_dev[k],
            device_id_type=MESH,
        )

    def bcopy(l, k):
        return pltpu.make_async_remote_copy(
            src_ref=bsrc.at[l, pl.ds(k * HALO, HALO)],
            dst_ref=ret.at[l, pl.ds(k * HALO, HALO)],
            send_sem=bs.at[l, k],
            recv_sem=br.at[l, k],
            device_id=in_dev[k],
            device_id_type=MESH,
        )

    def send_halo(l):
        for k in range(4):
            @pl.when(out_ok[k])
            def _(k=k):
                fcopy(l, k).start()

    def wait_halo(l):
        for k in range(4):
            @pl.when(in_ok[k])
            def _(k=k):
                fcopy(l, k).wait_recv()

    def send_ret(l):
        for k in range(4):
            @pl.when(in_ok[k])
            def _(k=k):
                bcopy(l, k).start()

    def wait_ret(l):
        for k in range(4):
            @pl.when(out_ok[k])
            def _(k=k):
                bcopy(l, k).wait_recv()

    def acopy(l, off):
        peer = lax.rem(d + off, D)
        return pltpu.make_async_remote_copy(
            src_ref=grads.at[l, pl.ds(pl.multiple_of(peer * share, share), share)],
            dst_ref=buf_a.at[l, off - 1],
            send_sem=a_s.at[l, off - 1],
            recv_sem=a_r.at[l, off - 1],
            device_id={"dom": peer},
            device_id_type=MESH,
        )

    def b_copy(l, off):
        peer = lax.rem(g + off, G)
        return pltpu.make_async_remote_copy(
            src_ref=buf_b.at[l, g],
            dst_ref=buf_b.at[l, g],
            send_sem=b_s.at[l, off - 1],
            recv_sem=b_r.at[l, off - 1],
            device_id={"group": peer},
            device_id_type=MESH,
        )

    def c_copy(l, off):
        peer = lax.rem(d + off, D)
        mine = pl.ds(pl.multiple_of(d * share, share), share)
        return pltpu.make_async_remote_copy(
            src_ref=gat.at[l, mine],
            dst_ref=gat.at[l, mine],
            send_sem=c_s.at[l, off - 1],
            recv_sem=c_r.at[l, off - 1],
            device_id={"dom": peer},
            device_id_type=MESH,
        )

    for l in range(L):
        tab[l, N:, :] = jnp.zeros((4 * HALO, H), BF16)
        ret[l] = jnp.zeros((4 * HALO, H), BF16)
    barrier = pltpu.get_barrier_semaphore()
    for off in range(1, D):
        pl.semaphore_signal(
            barrier, inc=1, device_id={"dom": lax.rem(d + off, D)}, device_id_type=MESH
        )
    for off in range(1, G):
        pl.semaphore_signal(
            barrier, inc=1, device_id={"group": lax.rem(g + off, G)}, device_id_type=MESH
        )

    def spread_column(row):
        return jnp.broadcast_to(row, (128, row.shape[1])).T

    def one_hot(column, width, ref, row0):
        rows = column.shape[0]
        lane = lax.broadcasted_iota(jnp.int32, (rows, 128), 1)
        for j in range(width // 128):
            ref[row0 : row0 + rows, j * 128 : (j + 1) * 128] = (
                (column - 128 * j == lane).astype(F32).astype(BF16)
            )

    def one_hot_t(row, height, ref, col0):
        cols = row.shape[1]
        sub = lax.broadcasted_iota(jnp.int32, (128, cols), 0)
        for j in range(height // 128):
            ref[j * 128 : (j + 1) * 128, col0 : col0 + cols] = (
                (row - 128 * j == sub).astype(F32).astype(BF16)
            )

    x0 = nodes[0]
    tab[0, :N, :] = x0
    for k in range(4):
        one_hot(spread_column(sidx[0, k : k + 1, :]), N, o_x, k * HALO)
    fsrc[0] = mm(o_x[...], x0).astype(BF16)
    pl.semaphore_wait(barrier, D - 1 + G - 1)
    send_halo(0)

    for k in range(4):
        one_hot_t(sidx[0, k : k + 1, :], N, ot_x, k * HALO)
    sids = snd[...]
    past = sids - N
    edge_0 = cnt[0, 0]
    edge_1 = edge_0 + cnt[0, 1]
    edge_2 = edge_1 + cnt[0, 2]
    sids = (
        sids
        + jnp.where(past >= edge_0, HALO - cnt[0, 0], 0)
        + jnp.where(past >= edge_1, HALO - cnt[0, 1], 0)
        + jnp.where(past >= edge_2, HALO - cnt[0, 2], 0)
    )
    rids = rcv[...]
    for i in range(E // 256):
        part = slice(i * 256, (i + 1) * 256)
        one_hot(spread_column(rids[:, part]), N, o_r, i * 256)
        one_hot(spread_column(sids[:, part]), N + 4 * HALO, o_s, i * 256)
        one_hot_t(rids[:, part], N, ot_r, i * 256)
        one_hot_t(sids[:, part], N + 4 * HALO, ot_s, i * 256)

    for l in range(L):
        wait_halo(l)

        def edge_step(i, carry, l=l):
            rows = pl.ds(pl.multiple_of(i * C, C), C)
            e_rows = edges[0, rows, :] if l == 0 else e_in[l - 1, rows, :]
            s_rows = mm(o_s[rows, :], tab[l]).astype(BF16)
            q_rows = mm(o_r[rows, :], tab[l, :N, :]).astype(BF16)
            pair = jnp.concatenate([s_rows, q_rows], axis=1)
            sq[l, rows, :] = pair
            pre = mm(e_rows, w1[l, :H, :]) + mm(pair, w1[l, H:, :]) + bias[l, 0:1, :]
            h_rows, sl = silu_parts(pre)
            hid[l, rows, :] = h_rows
            slope[l, rows, :] = sl
            hat_rows, inv_rows = norm_parts(mm(h_rows, w2[l]) + bias[l, 1:2, :])
            hat[l, rows, :] = hat_rows
            inv[l, rows, :] = jnp.broadcast_to(inv_rows, hat_rows.shape)
            new = (e_rows.astype(F32) + hat_rows * gain[l, 0:1, :]).astype(BF16)
            if l + 1 < L:
                e_in[l, rows, :] = new
            else:
                e_last[rows, :] = new
            return carry

        lax.fori_loop(0, E // C, edge_step, 0)
        e_new = e_in[l] if l + 1 < L else e_last[...]
        x_rows = tab[l, :N, :]
        joined = jnp.concatenate([x_rows, mm(ot_r[...], e_new).astype(BF16)], axis=1)
        jn[l] = joined
        h_rows, sl = silu_parts(mm(joined, n1[l]) + bias[l, 2:3, :])
        nhid[l] = h_rows
        nslope[l] = sl
        hat_rows, inv_rows = norm_parts(mm(h_rows, n2[l]) + bias[l, 3:4, :])
        nhat[l] = hat_rows
        ninv[l] = jnp.broadcast_to(inv_rows, hat_rows.shape)
        x_new = (x_rows.astype(F32) + hat_rows * gain[l, 1:2, :]).astype(BF16)
        if l + 1 < L:
            tab[l + 1, :N, :] = x_new
            fsrc[l + 1] = mm(o_x[...], x_new).astype(BF16)
            send_halo(l + 1)
        else:
            x_out[0] = x_new

    for l in reversed(range(L)):
        cot = ncot[0].astype(F32) if l == L - 1 else x_cot.astype(F32)
        nh = nhat[l]
        dgn = fold(cot * nh)
        dmn = norm_back(cot, gain[l, 1:2, :], nh, ninv[l])
        dbn2 = fold(dmn)
        dmn = dmn.astype(BF16)
        dpn = mm_nt(dmn, n2[l]).astype(BF16).astype(F32) * nslope[l]
        dbn1 = fold(dpn)
        dpn = dpn.astype(BF16)
        djn = mm_nt(dpn, n1[l]).astype(BF16)
        dx[...] = cot + djn[:, :H].astype(F32)
        dab[...] = djn[:, H:]

        def edge_back(i, carry, l=l):
            s_g, s_b2, s_b1 = carry
            rows = pl.ds(pl.multiple_of(i * C, C), C)
            c_rows = mm(o_r[rows, :], dab[...])
            if l < L - 1:
                c_rows = (de[rows, :].astype(F32) + c_rows).astype(BF16).astype(F32)
            hat_rows = hat[l, rows, :]
            dm_rows = norm_back(c_rows, gain[l, 0:1, :], hat_rows, inv[l, rows, :])
            s_g = s_g + fold(c_rows * hat_rows)
            s_b2 = s_b2 + fold(dm_rows)
            dm_b = dm_rows.astype(BF16)
            dm[rows, :] = dm_b
            dp_rows = mm_nt(dm_b, w2[l]).astype(BF16).astype(F32) * slope[l, rows, :]
            s_b1 = s_b1 + fold(dp_rows)
            dp_b = dp_rows.astype(BF16)
            dp[rows, :] = dp_b
            dj = mm_nt(dp_b, w1[l]).astype(BF16)
            back = (c_rows + dj[:, :H].astype(F32)).astype(BF16)
            if l == 0:
                e_grad[0, rows, :] = back
            else:
                de[rows, :] = back
            dsq[rows, :] = dj[:, H:]
            return s_g, s_b2, s_b1

        zero = jnp.zeros((8, H), F32)
        dge, dbe2, dbe1 = lax.fori_loop(0, E // C, edge_back, (zero, zero, zero))
        bsrc[l] = mm(ot_s[N:, :], dsq[:, :H]).astype(BF16)
        send_ret(l)

        def put(first, value):
            grads[l, first : first + value.shape[0], :] = value.astype(BF16)

        dp_t = dp[...].T
        e_rows = edges[0] if l == 0 else e_in[l - 1]
        put(0, mm(dp_t, e_rows).T)
        put(H, mm(dp_t, sq[l]).T)
        put(3 * H, mm(dm[...].T, hid[l]).T)
        put(4 * H, mm(dpn.T, jn[l]).T)
        put(6 * H, mm(dmn.T, nhid[l]).T)
        small = [row_sum(v) for v in (dbe1, dbe2, dbn1, dbn2, dge, dgn)]
        put(
            rows_w,
            jnp.concatenate(small + [jnp.zeros((D * share - rows_w - 6, H), F32)], axis=0),
        )
        for off in range(1, D):
            acopy(l, off).start()
        total = dx[...] + mm(ot_s[:N, :], dsq[:, :H]) + mm(ot_r[...], dsq[:, H:])
        wait_ret(l)
        x_cot = (total + mm(ot_x[...], ret[l])).astype(BF16)
    x_grad[0] = x_cot

    mine = pl.ds(pl.multiple_of(d * share, share), share)
    for l in reversed(range(L)):
        acc = grads[l, mine, :].astype(F32)
        for off in range(1, D):
            acopy(l, off).wait_recv()
            acc = acc + buf_a[l, off - 1].astype(F32)
        buf_b[l, g] = acc.astype(BF16)
        for off in range(1, G):
            b_copy(l, off).start()
    for l in reversed(range(L)):
        for off in range(1, G):
            b_copy(l, off).wait_recv()
        acc = buf_b[l, 0].astype(F32)
        for i in range(1, G):
            acc = acc + buf_b[l, i].astype(F32)
        gat[l, mine, :] = acc.astype(BF16)
        for off in range(1, D):
            c_copy(l, off).start()
    scale = (D * G * N) ** (-0.5)
    for l in reversed(range(L)):
        for off in range(1, D):
            c_copy(l, off).wait_recv()

        def take(first, count):
            return gat[l, first : first + count, :].astype(F32) * scale

        g_w1[l] = take(0, 3 * H)
        g_w2[l] = take(3 * H, H)
        g_n1[l] = take(4 * H, 2 * H)
        g_n2[l] = take(6 * H, H)
        tail = take(rows_w, 16)
        g_b[l] = tail[:4]
        g_g[l] = tail[4:6]

    for l in range(L):
        for k in range(4):
            @pl.when(out_ok[k])
            def _(k=k, l=l):
                fcopy(l, k).wait_send()

            @pl.when(in_ok[k])
            def _(k=k, l=l):
                bcopy(l, k).wait_send()
        for off in range(1, D):
            acopy(l, off).wait_send()
            c_copy(l, off).wait_send()
        for off in range(1, G):
            b_copy(l, off).wait_send()


def shards(D, G, nodes, edges, node_cot, send_index, halo_count, senders, receivers, *weights):
    edge_in_w, edge_out_w, node_in_w, node_out_w, biases, gains = weights
    _, N, H = nodes.shape
    E = edges.shape[1]
    L = edge_in_w.shape[0]
    HALO = send_index.shape[2]
    C = 256
    rows = 7 * H + 6
    share = -(-rows // (16 * D)) * 16
    dims = (D, G, L, N, E, H, HALO, C, share)
    T = N + 4 * HALO
    R = D * share
    out_shape = (
        jax.ShapeDtypeStruct(nodes.shape, BF16),
        jax.ShapeDtypeStruct(nodes.shape, BF16),
        jax.ShapeDtypeStruct(edges.shape, BF16),
        jax.ShapeDtypeStruct(edge_in_w.shape, F32),
        jax.ShapeDtypeStruct(edge_out_w.shape, F32),
        jax.ShapeDtypeStruct(node_in_w.shape, F32),
        jax.ShapeDtypeStruct(node_out_w.shape, F32),
        jax.ShapeDtypeStruct(biases.shape, F32),
        jax.ShapeDtypeStruct(gains.shape, F32),
    )
    V = pltpu.VMEM
    dma = pltpu.SemaphoreType.DMA
    scratch = [
        V((E, T), BF16),
        V((T, E), BF16),
        V((E, N), BF16),
        V((N, E), BF16),
        V((4 * HALO, N), BF16),
        V((N, 4 * HALO), BF16),
        V((L, T, H), BF16),
        V((max(L - 1, 1), E, H), BF16),
        V((E, H), BF16),
        V((L, E, 2 * H), BF16),
        V((L, E, H), BF16),
        V((L, E, H), F32),
        V((L, E, H), F32),
        V((L, E, H), F32),
        V((L, N, 2 * H), BF16),
        V((L, N, H), BF16),
        V((L, N, H), F32),
        V((L, N, H), F32),
        V((L, N, H), F32),
        V((E, H), BF16),
        V((E, H), BF16),
        V((E, H), BF16),
        V((E, 2 * H), BF16),
        V((N, H), F32),
        V((N, H), BF16),
        V((L, 4 * HALO, H), BF16),
        V((L, 4 * HALO, H), BF16),
        V((L, 4 * HALO, H), BF16),
        V((L, R, H), BF16),
        V((L, max(D - 1, 1), share, H), BF16),
        V((L, G, share, H), BF16),
        V((L, R, H), BF16),
        dma((L, 4)),
        dma((L, 4)),
        dma((L, 4)),
        dma((L, 4)),
        dma((L, D)),
        dma((L, D)),
        dma((L, G)),
        dma((L, G)),
        dma((L, D)),
        dma((L, D)),
    ]
    vm = pl.BlockSpec(memory_space=pltpu.VMEM)
    sm = pl.BlockSpec(memory_space=pltpu.SMEM)
    return pl.pallas_call(
        functools.partial(kernel, dims),
        out_shape=out_shape,
        in_specs=[sm] + [vm] * 12,
        out_specs=tuple([vm] * 9),
        scratch_shapes=scratch,
        compiler_params=pltpu.CompilerParams(
            collective_id=0, has_side_effects=True, vmem_limit_bytes=56 * 1024 * 1024
        ),
    )(
        halo_count,
        nodes,
        edges,
        node_cot,
        send_index,
        senders,
        receivers,
        *weights,
    )


def solution(mesh):
    part3 = P(("dom", "group"), None, None)
    part2 = P(("dom", "group"), None)
    in_specs = (part3, part3, part3, part3, part2, part2, part2) + (P(),) * 6
    out_specs = (part3, part3, part3) + (P(),) * 6
    body = functools.partial(shards, mesh.shape["dom"], mesh.shape["group"])
    return jax.shard_map(
        body, mesh=mesh, in_specs=in_specs, out_specs=out_specs, check_vma=False
    )
```

time: 414 us -> 62.8 us (0.15); the launches traced: 407 us -> 62.4 us
  waiting for transfers between devices: 137 us -> 0 us
  other arithmetic: 79.1 us -> 0 us
  local copies, waits for them, and re-layouts: 84.7 us -> 8.89 us
  Pallas kernels: 0 us -> 52.9 us
  starting transfers between devices: 41 us -> 0 us
  matrix products: 32 us -> 0 us
  between operations: 17.6 us -> 0.67 us
  loops' own time: 15.7 us -> 0 us
    unnamed x5 -> x0, waiting for transfers between devices: 93.8 us -> none
    scatter-add x8 -> x0, other arithmetic: 53.9 us -> none  [the longest x2 21.1 us: local_layer(): recv_feat = table[receiver_ids].astype(jnp.bfloat16)]
    pallas_call x0 -> x1, Pallas kernels: none -> 52.9 us  [shards(): pl.pallas_call(functools.partial(kernel, dims), out_shape=out_shape, in_s...]
    ppermute x16 -> x0, starting transfers between devices: 40.9 us -> none  [the longest x8 30.2 us: padded(): before = lax.ppermute(last, axis, up)]
    psum x1 -> x0, waiting for transfers between devices: 35.8 us -> none  [reduce_grads(): shares = lax.psum(shares, 'group')]
    dot_general x36 -> x0, matrix products: 32 us -> none  [the longest x12 14.2 us: add_block(): lax.dot_general(onehot, block_rows, (((0,), (0,)), ((), ())), preferred_e...]
    gather x14 -> x0, local copies, waits for them, and re-layouts: 19.7 us -> none  [the longest x4 6.77 us: local_layer(): sent_feat = table[sender_ids].astype(jnp.bfloat16)]
    another operation x4 -> x0, loops' own time: 15.7 us -> none  [aggregate(): return lax.fori_loop(0, block_count, add_block, totals)]
  transfers between devices with their start and end apart: 19 -> 0, of which waited for: 6 -> 0; matrix products, arithmetic and copies ran while one was open for 4% -> 0% of each run, Pallas kernels for 0% -> 0%
where the time goes in v1:
time: 62.8 us; the launch traced here: 62.4 us
  Pallas kernels  52.9 us (84%)
  local copies, waits for them, and re-layouts  8.89 us (14%)
  between operations  0.67 us (1%)
    pallas_call x1, Pallas kernels, shards(): pl.pallas_call(functools.partial(kernel, dims), out_shape=out_shape, in_s...  52.9 us
    unnamed x23, local copies, waits for them, and re-layouts  8.89 us

profile of v1, /device:TPU:0, one launch (start us, length us, event | category | flops | bytes accessed | tf_op | source)
XLA Modules:
  0.0 62.4 jit_solution(353812211213941743)
XLA Ops:
  0.6 52.9 %shard_map.196 = (bf16[1,256,128]{2,1,0:T(8,128)(2,1)}, bf16[1,256,128]{2,1,0:T(8,128)(2,1)}, bf16[1,1536,128]{2,1,0:T(8,128)(2,1)}, f32[2,384,128]{2,1,0:T(8,12...) custom-call(s32[1,4]{1,0:T(1,128)} %cnt.1, ...), custom_call_target="tpu_custom_call" | custom-call | tf_op jit(solution)/shard_map/pallas_call | solution.py:502
  53.5 0.0 copy-start.4
  53.5 1.5 %copy.31 = bf16[1,256,128]{2,1,0:T(8,128)(2,1)} copy(bf16[1,256,128]{2,1,0:T(8,128)(2,1)} %get-tuple-element.18) | data formatting | bytes 131072
  55.0 0.0 copy-done.4
  55.0 0.6 %copy.32 = bf16[1,256,128]{2,1,0:T(8,128)(2,1)} copy(bf16[1,256,128]{2,1,0:T(8,128)(2,1)S(1)} %copy-done.4) | data formatting | bytes 131072
  55.7 0.0 copy-start
  55.7 1.8 %copy.33 = bf16[1,1536,128]{2,1,0:T(8,128)(2,1)} copy(bf16[1,1536,128]{2,1,0:T(8,128)(2,1)} %get-tuple-element.20) | data formatting | bytes 786432
  57.5 0.0 copy-done
  57.5 0.0 copy-start.3
  57.5 0.7 %copy.34 = f32[2,384,128]{2,1,0:T(8,128)} copy(f32[2,384,128]{2,1,0:T(8,128)S(1)} %copy-done) | data formatting | bytes 786432
  58.2 0.3 copy-done.3
  58.5 0.0 copy-start.1
  58.5 0.7 %copy.35 = f32[2,128,128]{2,1,0:T(8,128)} copy(f32[2,128,128]{2,1,0:T(8,128)S(1)} %copy-done.3) | data formatting | bytes 262144
  59.2 0.3 copy-done.1
  59.5 0.0 copy-start.2
  59.5 0.7 %copy.36 = f32[2,256,128]{2,1,0:T(8,128)} copy(f32[2,256,128]{2,1,0:T(8,128)S(1)} %copy-done.1) | data formatting | bytes 524288
  60.2 0.3 copy-done.2
  60.5 0.0 copy-start.5
  60.5 0.7 %copy.37 = f32[2,128,128]{2,1,0:T(8,128)} copy(f32[2,128,128]{2,1,0:T(8,128)S(1)} %copy-done.2) | data formatting | bytes 262144
  61.2 0.0 copy-done.5
  61.2 0.0 copy-start.6
  61.2 0.6 copy.38
  61.8 0.1 copy-done.6
  61.9 0.6 copy.39
Async XLA Ops:
  53.5 1.5 %copy-start.4 = (bf16[1,256,128]{2,1,0:T(8,128)(2,1)S(1)}, bf16[1,256,128]{2,1,0:T(8,128)(2,1)}, u32[]{:S(2)}) copy-start(bf16[1,256,128]{2,1,0:T(8,128)(2,1)} %get-tuple-element.19) | copy-start | bytes 196612
  55.7 1.8 %copy-start = (f32[2,384,128]{2,1,0:T(8,128)S(1)}, f32[2,384,128]{2,1,0:T(8,128)}, u32[]{:S(2)}) copy-start(f32[2,384,128]{2,1,0:T(8,128)} %get-tuple-element.21) | copy-start | bytes 1179652
  57.5 1.0 %copy-start.3 = (f32[2,128,128]{2,1,0:T(8,128)S(1)}, f32[2,128,128]{2,1,0:T(8,128)}, u32[]{:S(2)}) copy-start(f32[2,128,128]{2,1,0:T(8,128)} %get-tuple-element.22) | copy-start | bytes 393220
  58.5 1.0 %copy-start.1 = (f32[2,256,128]{2,1,0:T(8,128)S(1)}, f32[2,256,128]{2,1,0:T(8,128)}, u32[]{:S(2)}) copy-start(f32[2,256,128]{2,1,0:T(8,128)} %get-tuple-element.23) | copy-start | bytes 786436
  59.5 1.0 %copy-start.2 = (f32[2,128,128]{2,1,0:T(8,128)S(1)}, f32[2,128,128]{2,1,0:T(8,128)}, u32[]{:S(2)}) copy-start(f32[2,128,128]{2,1,0:T(8,128)} %get-tuple-element.24) | copy-start | bytes 393220
  60.5 0.7 %copy-start.5 = (f32[2,4,128]{2,1,0:T(4,128)S(1)}, f32[2,4,128]{2,1,0:T(4,128)}, u32[]{:S(2)}) copy-start(f32[2,4,128]{2,1,0:T(4,128)} %get-tuple-element.25) | copy-start | bytes 12292
  61.2 0.7 %copy-start.6 = (f32[2,2,128]{2,1,0:T(2,128)S(1)}, f32[2,2,128]{2,1,0:T(2,128)}, u32[]{:S(2)}) copy-start(f32[2,2,128]{2,1,0:T(2,128)} %get-tuple-element.26) | copy-start | bytes 6148

commit v2 on v1

--- a/solution.py
+++ b/solution.py
@@ -10,6 +10,7 @@
 F32 = jnp.float32
 BF16 = jnp.bfloat16
 MESH = pl.DeviceIdType.MESH
+VMEM_MAIN = 58 * 1024 * 1024
 
 
 def mm(a, b):
@@ -51,28 +52,24 @@
 
 def kernel(
     dims,
-    cnt,
-    nodes,
-    edges,
-    ncot,
-    sidx,
-    snd,
-    rcv,
-    w1,
-    w2,
-    n1,
-    n2,
-    bias,
-    gain,
+    cnt_h,
+    nodes_h,
+    edges_h,
+    ncot_h,
+    sidx_h,
+    snd_h,
+    rcv_h,
+    w1_h,
+    w2_h,
+    n1_h,
+    n2_h,
+    bias_h,
+    gain_h,
     x_out,
     x_grad,
     e_grad,
-    g_w1,
-    g_w2,
-    g_n1,
-    g_n2,
-    g_b,
-    g_g,
+    sum_n,
+    sum_e,
     o_s,
     ot_s,
     o_r,
@@ -101,10 +98,14 @@
     fsrc,
     bsrc,
     ret,
-    grads,
-    buf_a,
-    buf_b,
-    gat,
+    grads_n,
+    buf_an,
+    buf_bn,
+    gat_n,
+    grads_e,
+    buf_ae,
+    buf_be,
+    gat_e,
     fs,
     fr,
     bs,
@@ -115,11 +116,52 @@
     b_r,
     c_s,
     c_r,
+    cnt,
+    nodes,
+    edges,
+    ncot,
+    sidx,
+    snd,
+    rcv,
+    w1,
+    w2,
+    n1,
+    n2,
+    bias,
+    gain,
+    in_sem,
 ):
-    D, G, L, N, E, H, HALO, C, share = dims
+    D, G, L, N, E, H, HALO, C, share_n, share_e = dims
+    shares = (share_n, share_e)
+    grads = (grads_n, grads_e)
+    buf_a = (buf_an, buf_ae)
+    buf_b = (buf_bn, buf_be)
+    gat = (gat_n, gat_e)
+    sums = (sum_n, sum_e)
+    loads = [
+        pltpu.make_async_copy(src, dst, in_sem.at[i])
+        for i, (src, dst) in enumerate(
+            (
+                (nodes_h, nodes),
+                (sidx_h, sidx),
+                (snd_h, snd),
+                (rcv_h, rcv),
+                (cnt_h, cnt),
+                (edges_h, edges),
+                (w1_h, w1),
+                (w2_h, w2),
+                (bias_h, bias),
+                (gain_h, gain),
+                (n1_h, n1),
+                (n2_h, n2),
+                (ncot_h, ncot),
+            )
+        )
+    ]
+    for load in loads:
+        load.start()
     d = lax.axis_index("dom")
     g = lax.axis_index("group")
-    rows_w = 7 * H
 
     has_up = d + 1 < D
     has_down = d > 0
@@ -174,39 +216,68 @@
             def _(k=k):
                 bcopy(l, k).wait_recv()
 
-    def acopy(l, off):
+    def a_copy(t, l, off):
         peer = lax.rem(d + off, D)
         return pltpu.make_async_remote_copy(
-            src_ref=grads.at[l, pl.ds(pl.multiple_of(peer * share, share), share)],
-            dst_ref=buf_a.at[l, off - 1],
-            send_sem=a_s.at[l, off - 1],
-            recv_sem=a_r.at[l, off - 1],
+            src_ref=grads[t].at[l, peer],
+            dst_ref=buf_a[t].at[l, off - 1],
+            send_sem=a_s.at[t, l, off - 1],
+            recv_sem=a_r.at[t, l, off - 1],
             device_id={"dom": peer},
             device_id_type=MESH,
         )
 
-    def b_copy(l, off):
-        peer = lax.rem(g + off, G)
+    def b_copy(t, l, off):
         return pltpu.make_async_remote_copy(
-            src_ref=buf_b.at[l, g],
-            dst_ref=buf_b.at[l, g],
-            send_sem=b_s.at[l, off - 1],
-            recv_sem=b_r.at[l, off - 1],
-            device_id={"group": peer},
+            src_ref=buf_b[t].at[l, g],
+            dst_ref=buf_b[t].at[l, g],
+            send_sem=b_s.at[t, l, off - 1],
+            recv_sem=b_r.at[t, l, off - 1],
+            device_id={"group": lax.rem(g + off, G)},
             device_id_type=MESH,
         )
 
-    def c_copy(l, off):
-        peer = lax.rem(d + off, D)
-        mine = pl.ds(pl.multiple_of(d * share, share), share)
+    def c_copy(t, l, off):
         return pltpu.make_async_remote_copy(
-            src_ref=gat.at[l, mine],
-            dst_ref=gat.at[l, mine],
-            send_sem=c_s.at[l, off - 1],
-            recv_sem=c_r.at[l, off - 1],
-            device_id={"dom": peer},
+            src_ref=gat[t].at[l, d],
+            dst_ref=gat[t].at[l, d],
+            send_sem=c_s.at[t, l, off - 1],
+            recv_sem=c_r.at[t, l, off - 1],
+            device_id={"dom": lax.rem(d + off, D)},
             device_id_type=MESH,
         )
+
+    def start_a(t, l, pieces):
+        rows = sum(p.shape[0] for p in pieces)
+        pad = jnp.zeros((D * shares[t] - rows, H), F32)
+        whole = jnp.concatenate(list(pieces) + [pad], axis=0)
+        grads[t][l] = whole.reshape(D, shares[t], H).astype(BF16)
+        for off in range(1, D):
+            a_copy(t, l, off).start()
+
+    def start_b(t, l):
+        acc = grads[t][l, d].astype(F32)
+        for off in range(1, D):
+            a_copy(t, l, off).wait_recv()
+            acc = acc + buf_a[t][l, off - 1].astype(F32)
+        buf_b[t][l, g] = acc.astype(BF16)
+        for off in range(1, G):
+            b_copy(t, l, off).start()
+
+    def start_c(t, l):
+        for off in range(1, G):
+            b_copy(t, l, off).wait_recv()
+        acc = buf_b[t][l, 0].astype(F32)
+        for i in range(1, G):
+            acc = acc + buf_b[t][l, i].astype(F32)
+        gat[t][l, d] = acc.astype(BF16)
+        for off in range(1, D):
+            c_copy(t, l, off).start()
+
+    def end_c(t, l):
+        for off in range(1, D):
+            c_copy(t, l, off).wait_recv()
+        sums[t][l] = gat[t][l]
 
     for l in range(L):
         tab[l, N:, :] = jnp.zeros((4 * HALO, H), BF16)
@@ -240,6 +311,8 @@
                 (row - 128 * j == sub).astype(F32).astype(BF16)
             )
 
+    loads[0].wait()
+    loads[1].wait()
     x0 = nodes[0]
     tab[0, :N, :] = x0
     for k in range(4):
@@ -250,6 +323,8 @@
 
     for k in range(4):
         one_hot_t(sidx[0, k : k + 1, :], N, ot_x, k * HALO)
+    for load in loads[2:5]:
+        load.wait()
     sids = snd[...]
     past = sids - N
     edge_0 = cnt[0, 0]
@@ -269,17 +344,30 @@
         one_hot_t(rids[:, part], N, ot_r, i * 256)
         one_hot_t(sids[:, part], N + 4 * HALO, ot_s, i * 256)
 
+    for load in loads[5:]:
+        load.wait()
+
     for l in range(L):
+        def own_step(i, carry, l=l):
+            rows = pl.ds(pl.multiple_of(i * C, C), C)
+            e_rows = edges[0, rows, :] if l == 0 else e_in[l - 1, rows, :]
+            sq[l, rows, :H] = mm(o_s[rows, :N], tab[l, :N, :]).astype(BF16)
+            q_rows = mm(o_r[rows, :], tab[l, :N, :]).astype(BF16)
+            sq[l, rows, H:] = q_rows
+            slope[l, rows, :] = (
+                mm(e_rows, w1[l, :H, :]) + mm(q_rows, w1[l, 2 * H :, :]) + bias[l, 0:1, :]
+            )
+            return carry
+
+        lax.fori_loop(0, E // C, own_step, 0)
         wait_halo(l)
 
         def edge_step(i, carry, l=l):
             rows = pl.ds(pl.multiple_of(i * C, C), C)
             e_rows = edges[0, rows, :] if l == 0 else e_in[l - 1, rows, :]
-            s_rows = mm(o_s[rows, :], tab[l]).astype(BF16)
-            q_rows = mm(o_r[rows, :], tab[l, :N, :]).astype(BF16)
-            pair = jnp.concatenate([s_rows, q_rows], axis=1)
-            sq[l, rows, :] = pair
-            pre = mm(e_rows, w1[l, :H, :]) + mm(pair, w1[l, H:, :]) + bias[l, 0:1, :]
+            s_rows = sq[l, rows, :H] + mm(o_s[rows, N:], tab[l, N:, :]).astype(BF16)
+            sq[l, rows, :H] = s_rows
+            pre = slope[l, rows, :] + mm(s_rows, w1[l, H : 2 * H, :])
             h_rows, sl = silu_parts(pre)
             hid[l, rows, :] = h_rows
             slope[l, rows, :] = sl
@@ -325,6 +413,14 @@
         djn = mm_nt(dpn, n1[l]).astype(BF16)
         dx[...] = cot + djn[:, :H].astype(F32)
         dab[...] = djn[:, H:]
+        start_a(
+            0,
+            l,
+            [mm(dpn.T, jn[l]).T, mm(dmn.T, nhid[l]).T]
+            + [row_sum(v) for v in (dbn1, dbn2, dgn)],
+        )
+        if l + 1 < L:
+            start_b(0, l + 1)
 
         def edge_back(i, carry, l=l):
             s_g, s_b2, s_b1 = carry
@@ -353,64 +449,40 @@
 
         zero = jnp.zeros((8, H), F32)
         dge, dbe2, dbe1 = lax.fori_loop(0, E // C, edge_back, (zero, zero, zero))
-        bsrc[l] = mm(ot_s[N:, :], dsq[:, :H]).astype(BF16)
-        send_ret(l)
-
-        def put(first, value):
-            grads[l, first : first + value.shape[0], :] = value.astype(BF16)
-
+        def halo_cots():
+            bsrc[l] = mm(ot_s[N:, :], dsq[:, :H]).astype(BF16)
+            send_ret(l)
+
+        if l > 0:
+            halo_cots()
+        if l + 1 < L:
+            start_b(1, l + 1)
         dp_t = dp[...].T
         e_rows = edges[0] if l == 0 else e_in[l - 1]
-        put(0, mm(dp_t, e_rows).T)
-        put(H, mm(dp_t, sq[l]).T)
-        put(3 * H, mm(dm[...].T, hid[l]).T)
-        put(4 * H, mm(dpn.T, jn[l]).T)
-        put(6 * H, mm(dmn.T, nhid[l]).T)
-        small = [row_sum(v) for v in (dbe1, dbe2, dbn1, dbn2, dge, dgn)]
-        put(
-            rows_w,
-            jnp.concatenate(small + [jnp.zeros((D * share - rows_w - 6, H), F32)], axis=0),
-        )
-        for off in range(1, D):
-            acopy(l, off).start()
+        start_a(
+            1,
+            l,
+            [mm(dp_t, e_rows).T, mm(dp_t, sq[l]).T, mm(dm[...].T, hid[l]).T]
+            + [row_sum(v) for v in (dbe1, dbe2, dge)],
+        )
+        if l == 0:
+            halo_cots()
         total = dx[...] + mm(ot_s[:N, :], dsq[:, :H]) + mm(ot_r[...], dsq[:, H:])
+        if l + 1 < L:
+            start_c(0, l + 1)
         wait_ret(l)
         x_cot = (total + mm(ot_x[...], ret[l])).astype(BF16)
     x_grad[0] = x_cot
 
-    mine = pl.ds(pl.multiple_of(d * share, share), share)
+    start_b(0, 0)
+    if L > 1:
+        start_c(1, 1)
+    start_b(1, 0)
+    start_c(0, 0)
+    start_c(1, 0)
     for l in reversed(range(L)):
-        acc = grads[l, mine, :].astype(F32)
-        for off in range(1, D):
-            acopy(l, off).wait_recv()
-            acc = acc + buf_a[l, off - 1].astype(F32)
-        buf_b[l, g] = acc.astype(BF16)
-        for off in range(1, G):
-            b_copy(l, off).start()
-    for l in reversed(range(L)):
-        for off in range(1, G):
-            b_copy(l, off).wait_recv()
-        acc = buf_b[l, 0].astype(F32)
-        for i in range(1, G):
-            acc = acc + buf_b[l, i].astype(F32)
-        gat[l, mine, :] = acc.astype(BF16)
-        for off in range(1, D):
-            c_copy(l, off).start()
-    scale = (D * G * N) ** (-0.5)
-    for l in reversed(range(L)):
-        for off in range(1, D):
-            c_copy(l, off).wait_recv()
-
-        def take(first, count):
-            return gat[l, first : first + count, :].astype(F32) * scale
-
-        g_w1[l] = take(0, 3 * H)
-        g_w2[l] = take(3 * H, H)
-        g_n1[l] = take(4 * H, 2 * H)
-        g_n2[l] = take(6 * H, H)
-        tail = take(rows_w, 16)
-        g_b[l] = tail[:4]
-        g_g[l] = tail[4:6]
+        for t in range(2):
+            end_c(t, l)
 
     for l in range(L):
         for k in range(4):
@@ -421,11 +493,33 @@
             @pl.when(in_ok[k])
             def _(k=k, l=l):
                 bcopy(l, k).wait_send()
-        for off in range(1, D):
-            acopy(l, off).wait_send()
-            c_copy(l, off).wait_send()
-        for off in range(1, G):
-            b_copy(l, off).wait_send()
+        for t in range(2):
+            for off in range(1, D):
+                a_copy(t, l, off).wait_send()
+                c_copy(t, l, off).wait_send()
+            for off in range(1, G):
+                b_copy(t, l, off).wait_send()
+
+
+def finish(scale, H, x0, xg0, eg0, sum_n, sum_e, x1, xg1, eg1, g_w1, g_w2, g_n1, g_n2, g_b, g_g):
+    x1[...] = x0[...]
+    xg1[...] = xg0[...]
+    eg1[...] = eg0[...]
+    L, D, share_n, _ = sum_n.shape
+    share_e = sum_e.shape[2]
+    for l in range(L):
+        node = (sum_n[l].astype(F32) * scale).reshape(D * share_n, H)
+        edge = (sum_e[l].astype(F32) * scale).reshape(D * share_e, H)
+        g_n1[l] = node[: 2 * H]
+        g_n2[l] = node[2 * H : 3 * H]
+        g_w1[l] = edge[: 3 * H]
+        g_w2[l] = edge[3 * H : 4 * H]
+        node = node[3 * H : 3 * H + 8]
+        edge = edge[4 * H : 4 * H + 8]
+        g_b[l, 0:2, :] = edge[0:2]
+        g_b[l, 2:4, :] = node[0:2]
+        g_g[l, 0:1, :] = edge[2:3]
+        g_g[l, 1:2, :] = node[2:3]
 
 
 def shards(D, G, nodes, edges, node_cot, send_index, halo_count, senders, receivers, *weights):
@@ -435,11 +529,17 @@
     L = edge_in_w.shape[0]
     HALO = send_index.shape[2]
     C = 256
-    rows = 7 * H + 6
-    share = -(-rows // (16 * D)) * 16
-    dims = (D, G, L, N, E, H, HALO, C, share)
+    share_n = -(-(3 * H + 3) // (8 * D)) * 8
+    share_e = -(-(4 * H + 3) // (8 * D)) * 8
+    dims = (D, G, L, N, E, H, HALO, C, share_n, share_e)
     T = N + 4 * HALO
-    R = D * share
+    own_shape = (
+        pltpu.VMEM(nodes.shape, BF16),
+        pltpu.VMEM(nodes.shape, BF16),
+        pltpu.VMEM(edges.shape, BF16),
+        pltpu.VMEM((L, D, share_n, H), BF16),
+        pltpu.VMEM((L, D, share_e, H), BF16),
+    )
     out_shape = (
         jax.ShapeDtypeStruct(nodes.shape, BF16),
         jax.ShapeDtypeStruct(nodes.shape, BF16),
@@ -482,42 +582,51 @@
         V((L, 4 * HALO, H), BF16),
         V((L, 4 * HALO, H), BF16),
         V((L, 4 * HALO, H), BF16),
-        V((L, R, H), BF16),
-        V((L, max(D - 1, 1), share, H), BF16),
-        V((L, G, share, H), BF16),
-        V((L, R, H), BF16),
+        V((L, D, share_n, H), BF16),
+        V((L, max(D - 1, 1), share_n, H), BF16),
+        V((L, G, share_n, H), BF16),
+        V((L, D, share_n, H), BF16),
+        V((L, D, share_e, H), BF16),
+        V((L, max(D - 1, 1), share_e, H), BF16),
+        V((L, G, share_e, H), BF16),
+        V((L, D, share_e, H), BF16),
         dma((L, 4)),
         dma((L, 4)),
         dma((L, 4)),
         dma((L, 4)),
-        dma((L, D)),
-        dma((L, D)),
-        dma((L, G)),
-        dma((L, G)),
-        dma((L, D)),
-        dma((L, D)),
+        dma((2, L, D)),
+        dma((2, L, D)),
+        dma((2, L, G)),
+        dma((2, L, G)),
+        dma((2, L, D)),
+        dma((2, L, D)),
+        pltpu.SMEM(halo_count.shape, jnp.int32),
     ]
+    operands = (nodes, edges, node_cot, send_index, senders, receivers) + weights
+    scratch += [V(x.shape, x.dtype) for x in operands] + [dma((13,))]
     vm = pl.BlockSpec(memory_space=pltpu.VMEM)
-    sm = pl.BlockSpec(memory_space=pltpu.SMEM)
-    return pl.pallas_call(
+    hbm = pl.BlockSpec(memory_space=pltpu.HBM)
+    own = pl.pallas_call(
         functools.partial(kernel, dims),
-        out_shape=out_shape,
-        in_specs=[sm] + [vm] * 12,
-        out_specs=tuple([vm] * 9),
+        out_shape=own_shape,
+        in_specs=[hbm] * 13,
+        out_specs=tuple([vm] * 5),
         scratch_shapes=scratch,
         compiler_params=pltpu.CompilerParams(
-            collective_id=0, has_side_effects=True, vmem_limit_bytes=56 * 1024 * 1024
+            collective_id=0, has_side_effects=True, vmem_limit_bytes=VMEM_MAIN
         ),
     )(
         halo_count,
-        nodes,
-        edges,
-        node_cot,
-        send_index,
-        senders,
-        receivers,
-        *weights,
+        *operands,
     )
+    scale = (D * G * N) ** (-0.5)
+    return pl.pallas_call(
+        functools.partial(finish, scale, H),
+        out_shape=out_shape,
+        in_specs=[vm] * 5,
+        out_specs=tuple([vm] * 9),
+        compiler_params=pltpu.CompilerParams(vmem_limit_bytes=8 * 1024 * 1024),
+    )(*own)
 
 
 def solution(mesh):

time: 62.8 us -> 51.3 us (0.82)
  local copies, waits for them, and re-layouts: 8.89 us -> 0 us
  Pallas kernels: 52.9 us -> 50.5 us
    unnamed x23 -> x0, local copies, waits for them, and re-layouts: 8.89 us -> none
    pallas_call x1 -> x2, Pallas kernels: 52.9 us -> 50.5 us  [the longest x1 49.3 us: shards(): pl.pallas_call(functools.partial(kernel, dims), out_shape=own_shape, in_s...]
where the time goes in v2:
time: 51.3 us; the launch traced here: 51.2 us
  Pallas kernels  50.5 us (98%)
  between operations  0.66 us (1%)
    pallas_call x1, Pallas kernels, shards(): pl.pallas_call(functools.partial(kernel, dims), out_shape=own_shape, in_s...  49.3 us
    pallas_call x1, Pallas kernels, shards(): pl.pallas_call(functools.partial(finish, scale, H), out_shape=out_shape,...  1.2 us

profile of v2, /device:TPU:0, one launch (start us, length us, event | category | flops | bytes accessed | tf_op | source)
XLA Modules:
  0.0 51.2 jit_solution(549817324721616130)
XLA Ops:
  0.6 49.3 %shard_map.196 = (bf16[1,256,128]{2,1,0:T(8,128)(2,1)S(1)}, bf16[1,256,128]{2,1,0:T(8,128)(2,1)S(1)}, bf16[1,1536,128]{2,1,0:T(8,128)(2,1)S(1)}, bf16[2,8,56,128...) custom-call(s32[1,4]{1,0:T(1,128)} %cnt_h.1, bf16[1,256,128]{2,1,0:T(8,128)(2,1)} %nodes_h.1, ...), custom_call_target="tpu_custom_call" | custom-call | tf_op jit(solution)/shard_map/pallas_call | solution.py:609
  50.0 1.2 %shard_map.197 = (bf16[1,256,128]{2,1,0:T(8,128)(2,1)}, bf16[1,256,128]{2,1,0:T(8,128)(2,1)}, bf16[1,1536,128]{2,1,0:T(8,128)(2,1)}, f32[2,384,128]{2,1,0:T(8,12...) custom-call(bf16[1,256,128]{2,1,0:T(8,128)(2,1)S(1)} %get-tuple-elem, ...), custom_call_target="tpu_custom_call" | custom-call | tf_op jit(solution)/shard_map/pallas_call | solution.py:623

commit v3 on v2

--- a/solution.py
+++ b/solution.py
@@ -46,7 +46,7 @@
 
 
 def silu_parts(pre):
-    sig = 1.0 / (1.0 + jnp.exp(-pre))
+    sig = 0.5 + 0.5 * jnp.tanh(0.5 * pre)
     return (pre * sig).astype(BF16), sig * (1.0 + pre * (1.0 - sig))
 
 
@@ -101,11 +101,9 @@
     grads_n,
     buf_an,
     buf_bn,
-    gat_n,
     grads_e,
     buf_ae,
     buf_be,
-    gat_e,
     fs,
     fr,
     bs,
@@ -136,8 +134,7 @@
     grads = (grads_n, grads_e)
     buf_a = (buf_an, buf_ae)
     buf_b = (buf_bn, buf_be)
-    gat = (gat_n, gat_e)
-    sums = (sum_n, sum_e)
+    gat = (sum_n, sum_e)
     loads = [
         pltpu.make_async_copy(src, dst, in_sem.at[i])
         for i, (src, dst) in enumerate(
@@ -277,7 +274,6 @@
     def end_c(t, l):
         for off in range(1, D):
             c_copy(t, l, off).wait_recv()
-        sums[t][l] = gat[t][l]
 
     for l in range(L):
         tab[l, N:, :] = jnp.zeros((4 * HALO, H), BF16)
@@ -321,8 +317,6 @@
     pl.semaphore_wait(barrier, D - 1 + G - 1)
     send_halo(0)
 
-    for k in range(4):
-        one_hot_t(sidx[0, k : k + 1, :], N, ot_x, k * HALO)
     for load in loads[2:5]:
         load.wait()
     sids = snd[...]
@@ -342,7 +336,6 @@
         one_hot(spread_column(rids[:, part]), N, o_r, i * 256)
         one_hot(spread_column(sids[:, part]), N + 4 * HALO, o_s, i * 256)
         one_hot_t(rids[:, part], N, ot_r, i * 256)
-        one_hot_t(sids[:, part], N + 4 * HALO, ot_s, i * 256)
 
     for load in loads[5:]:
         load.wait()
@@ -360,6 +353,12 @@
             return carry
 
         lax.fori_loop(0, E // C, own_step, 0)
+        if l == L - 1:
+            for k in range(4):
+                one_hot_t(sidx[0, k : k + 1, :], N, ot_x, k * HALO)
+            for i in range(E // 256):
+                part = slice(i * 256, (i + 1) * 256)
+                one_hot_t(sids[:, part], N + 4 * HALO, ot_s, i * 256)
         wait_halo(l)
 
         def edge_step(i, carry, l=l):
@@ -466,19 +465,18 @@
             + [row_sum(v) for v in (dbe1, dbe2, dge)],
         )
         if l == 0:
+            start_b(0, 0)
             halo_cots()
-        total = dx[...] + mm(ot_s[:N, :], dsq[:, :H]) + mm(ot_r[...], dsq[:, H:])
         if l + 1 < L:
             start_c(0, l + 1)
+            start_c(1, l + 1)
+        total = dx[...] + mm(ot_s[:N, :], dsq[:, :H]) + mm(ot_r[...], dsq[:, H:])
         wait_ret(l)
         x_cot = (total + mm(ot_x[...], ret[l])).astype(BF16)
     x_grad[0] = x_cot
 
-    start_b(0, 0)
-    if L > 1:
-        start_c(1, 1)
+    start_c(0, 0)
     start_b(1, 0)
-    start_c(0, 0)
     start_c(1, 0)
     for l in reversed(range(L)):
         for t in range(2):
@@ -528,7 +526,7 @@
     E = edges.shape[1]
     L = edge_in_w.shape[0]
     HALO = send_index.shape[2]
-    C = 256
+    C = 512
     share_n = -(-(3 * H + 3) // (8 * D)) * 8
     share_e = -(-(4 * H + 3) // (8 * D)) * 8
     dims = (D, G, L, N, E, H, HALO, C, share_n, share_e)
@@ -585,11 +583,9 @@
         V((L, D, share_n, H), BF16),
         V((L, max(D - 1, 1), share_n, H), BF16),
         V((L, G, share_n, H), BF16),
-        V((L, D, share_n, H), BF16),
         V((L, D, share_e, H), BF16),
         V((L, max(D - 1, 1), share_e, H), BF16),
         V((L, G, share_e, H), BF16),
-        V((L, D, share_e, H), BF16),
         dma((L, 4)),
         dma((L, 4)),
         dma((L, 4)),

time: 51.3 us -> 44.3 us (0.86)
  Pallas kernels: 50.5 us -> 43.5 us
    pallas_call x1, Pallas kernels: 49.3 us -> 42.3 us  [shards(): pl.pallas_call(functools.partial(kernel, dims), out_shape=own_shape, in_s...]
where the time goes in v3:
time: 44.3 us; the launch traced here: 44.1 us
  Pallas kernels  43.5 us (98%)
  between operations  0.66 us (1%)
    pallas_call x1, Pallas kernels, shards(): pl.pallas_call(functools.partial(kernel, dims), out_shape=own_shape, in_s...  42.3 us
    pallas_call x1, Pallas kernels, shards(): pl.pallas_call(functools.partial(finish, scale, H), out_shape=out_shape,...  1.2 us

profile of v3, /device:TPU:0, one launch (start us, length us, event | category | flops | bytes accessed | tf_op | source)
XLA Modules:
  0.0 44.1 jit_solution(7289837482282052211)
XLA Ops:
  0.6 42.3 %shard_map.196 = (bf16[1,256,128]{2,1,0:T(8,128)(2,1)S(1)}, bf16[1,256,128]{2,1,0:T(8,128)(2,1)S(1)}, bf16[1,1536,128]{2,1,0:T(8,128)(2,1)S(1)}, bf16[2,8,56,128...) custom-call(s32[1,4]{1,0:T(1,128)} %cnt_h.1, bf16[1,256,128]{2,1,0:T(8,128)(2,1)} %nodes_h.1, ...), custom_call_target="tpu_custom_call" | custom-call | tf_op jit(solution)/shard_map/pallas_call | solution.py:605
  42.9 1.2 %shard_map.197 = (bf16[1,256,128]{2,1,0:T(8,128)(2,1)}, bf16[1,256,128]{2,1,0:T(8,128)(2,1)}, bf16[1,1536,128]{2,1,0:T(8,128)(2,1)}, f32[2,384,128]{2,1,0:T(8,12...) custom-call(bf16[1,256,128]{2,1,0:T(8,128)(2,1)S(1)} %get-tuple-elem, ...), custom_call_target="tpu_custom_call" | custom-call | tf_op jit(solution)/shard_map/pallas_call | solution.py:619

commit v4 on v3

--- a/solution.py
+++ b/solution.py
@@ -526,7 +526,7 @@
     E = edges.shape[1]
     L = edge_in_w.shape[0]
     HALO = send_index.shape[2]
-    C = 512
+    C = E // 2
     share_n = -(-(3 * H + 3) // (8 * D)) * 8
     share_e = -(-(4 * H + 3) // (8 * D)) * 8
     dims = (D, G, L, N, E, H, HALO, C, share_n, share_e)

time: 44.3 us -> 42.8 us (0.966)
  Pallas kernels: 43.5 us -> 42 us
    pallas_call x1, Pallas kernels: 42.3 us -> 40.8 us  [shards(): pl.pallas_call(functools.partial(kernel, dims), out_shape=own_shape, in_s...]
where the time goes in v4:
time: 42.8 us; the launch traced here: 42.6 us
  Pallas kernels  42 us (98%)
  between operations  0.66 us (2%)
    pallas_call x1, Pallas kernels, shards(): pl.pallas_call(functools.partial(kernel, dims), out_shape=own_shape, in_s...  40.8 us
    pallas_call x1, Pallas kernels, shards(): pl.pallas_call(functools.partial(finish, scale, H), out_shape=out_shape,...  1.2 us

profile of v4, /device:TPU:0, one launch (start us, length us, event | category | flops | bytes accessed | tf_op | source)
XLA Modules:
  0.0 42.6 jit_solution(4981998264949011535)
XLA Ops:
  0.6 40.8 %shard_map.196 = (bf16[1,256,128]{2,1,0:T(8,128)(2,1)S(1)}, bf16[1,256,128]{2,1,0:T(8,128)(2,1)S(1)}, bf16[1,1536,128]{2,1,0:T(8,128)(2,1)S(1)}, bf16[2,8,56,128...) custom-call(s32[1,4]{1,0:T(1,128)} %cnt_h.1, bf16[1,256,128]{2,1,0:T(8,128)(2,1)} %nodes_h.1, ...), custom_call_target="tpu_custom_call" | custom-call | tf_op jit(solution)/shard_map/pallas_call | solution.py:605
  41.4 1.2 %shard_map.197 = (bf16[1,256,128]{2,1,0:T(8,128)(2,1)}, bf16[1,256,128]{2,1,0:T(8,128)(2,1)}, bf16[1,1536,128]{2,1,0:T(8,128)(2,1)}, f32[2,384,128]{2,1,0:T(8,12...) custom-call(bf16[1,256,128]{2,1,0:T(8,128)(2,1)S(1)} %get-tuple-elem, ...), custom_call_target="tpu_custom_call" | custom-call | tf_op jit(solution)/shard_map/pallas_call | solution.py:619
